TPU v7x, 32 devices: a whole 2x2x4 slice. The times are simulated.
32 devices in a mesh: grp: 4 (over z), mem: 8 (over y, x, core).
Axes of the slice: x: 2, y: 2, z: 4, core: 2. Of those that a mesh axis runs over, the one named last changes fastest.
Arguments:
- child_means: float32 [65536, 64], P(('grp', 'mem')), may hold values from -48 to 48
- child_variances: float32 [65536, 64], P(('grp', 'mem')), may hold values from 0.2 to 2
- virtual_counts: int32 [65536], P(('grp', 'mem')), may hold values from 1 to 4
- assignment: int32 [65536, 1], P(('grp', 'mem')), may hold values from 0 to 511
Outputs:
- parent_means: float32 [512, 64], P('mem')
- parent_variances: float32 [512, 64], P('mem')
- parent_weights: float32 [512], P('mem')
All inputs are finite; a program needn't handle non-finite values.
Results may differ from a plain program's by a relative error of at most 0.0003.
Values sent between devices are 32-bit elements; how exact they have to be, the bound alone decides.
A program may use at most 64 MiB of HBM per device.

v0:
```python
import math
import jax
import jax.numpy as jnp
from jax import lax
from jax.sharding import PartitionSpec as P

P_SIZE = 512
ITERS = 2


def child_features(means, variances):
    return jnp.concatenate([means, variances + means * means], axis=1)


def accumulate(features, extras, weigh):
    row_count = features.shape[0]
    block = math.gcd(row_count, 1024)
    turns = row_count // block
    pieces = (features.reshape(turns, block, features.shape[1]),) + tuple(
        (extra.reshape((turns, block) + extra.shape[1:]) for extra in extras)
    )

    def advance(carry, piece):
        weights = weigh(*piece)
        sums = carry[0] + lax.dot_general(
            weights,
            piece[0],
            (((0,), (0,)), ((), ())),
            precision=lax.Precision.HIGHEST,
            preferred_element_type=jnp.float32,
        )
        counts = carry[1] + jnp.sum(weights, axis=0)
        return ((sums, counts), None)

    start_sums = (
        jnp.zeros((P_SIZE, features.shape[1]), jnp.float32),
        jnp.zeros((P_SIZE,), jnp.float32),
    )
    return lax.scan(advance, start_sums, pieces)[0]


def maximize(counts, sums, total):
    width = sums.shape[1] // 2
    mass = counts + 1.0
    means = sums[:, :width] / mass[:, None]
    second = (sums[:, width:] + 1.0) / mass[:, None]
    return (means, second - means * means, mass / (total + P_SIZE))


def parent_table(means, variances, weights):
    inverse = 1.0 / variances
    table = jnp.concatenate([-2.0 * means * inverse, inverse], axis=1)
    offset = jnp.sum(jnp.log(2.0 * math.pi * variances) + means * means * inverse, axis=1)
    return (table, offset, jnp.log(weights))


def soft_weights(block_features, block_virtual, table, offset, log_weight):
    width = block_features.shape[1] // 2
    cross = lax.dot_general(
        block_features,
        table,
        (((1,), (1,)), ((), ())),
        precision=lax.Precision.HIGHEST,
        preferred_element_type=jnp.float32,
    )
    ell = -0.5 / width * (cross + offset[None, :])
    score = log_weight[None, :] + block_virtual[:, None] * ell
    top = jnp.max(score, axis=1, keepdims=True)
    expd = jnp.exp(score - top)
    resp = expd / jnp.sum(expd, axis=1, keepdims=True)
    return resp * block_virtual[:, None]


def shards(child_means, child_variances, virtual_counts, assignment):
    features = child_features(child_means, child_variances)
    virtual = virtual_counts.astype(jnp.float32)
    labels = jnp.arange(P_SIZE, dtype=jnp.int32)

    def initial_weights(block_features, block_virtual, block_assign):
        return (block_assign == labels[None, :]).astype(jnp.float32) * block_virtual[:, None]

    sums, counts = accumulate(features, (virtual, assignment), initial_weights)
    total = lax.psum(jnp.sum(virtual), ("grp", "mem"))

    def combine(local_sums, local_counts):
        shared = (
            lax.psum_scatter(local_sums, "mem", scatter_dimension=0, tiled=True),
            lax.psum_scatter(local_counts, "mem", scatter_dimension=0, tiled=True),
        )
        return lax.psum((shared[0], shared[1]), "grp")

    own_sums, own_counts = combine(sums, counts)
    means, variances, weights = maximize(own_counts, own_sums, total)
    for iteration in range(ITERS):
        all_means, all_variances, all_weights = (
            lax.all_gather(means, "mem", axis=0, tiled=True),
            lax.all_gather(variances, "mem", axis=0, tiled=True),
            lax.all_gather(weights, "mem", axis=0, tiled=True),
        )
        table, offset, log_weight = parent_table(all_means, all_variances, all_weights)

        def weigh(block_features, block_virtual):
            return soft_weights(block_features, block_virtual, table, offset, log_weight)

        sums, counts = accumulate(features, (virtual,), weigh)
        own_sums, own_counts = combine(sums, counts)
        means, variances, weights = maximize(own_counts, own_sums, total)
    return (means, variances, weights)


def solution(mesh):
    in_specs = (
        P(("grp", "mem"), None),
        P(("grp", "mem"), None),
        P(("grp", "mem")),
        P(("grp", "mem"), None),
    )
    out_specs = (P("mem", None), P("mem", None), P("mem"))
    return jax.shard_map(shards, mesh=mesh, in_specs=in_specs, out_specs=out_specs, check_vma=False)
```

profile of v0, /device:TPU:0, one launch (start us, length us, event | category | flops | bytes accessed | tf_op | source)
XLA Modules:
  0.0 293.5 jit_solution(11252077472539837460)
XLA Ops:
  7.2 0.0 reduce-scatter.4.cloned.1.call-start
  7.2 1.3 multiply_add_fusion.2
  8.5 1.2 pad_maximum_fusion
  9.7 0.3 copy.9
  10.1 8.4 %while.39 = (s32[]{:T(128)}, f32[512,128]{1,0:T(8,128)S(1)}, f32[512]{0:T(512)S(1)}, s32[2,1024,1]{1,2,0:T(1,128)S(1)}, f32[2,1024]{1,0:T(2,128)S(1)}, /*index=5*/f32[2,1024,128]{2,1,0:T(8,128)S(1)}, s32[]{:T(128)}, s32[]{:T(128)}) while((s32[]{:T(128)}, f32[512,128]{1,0:T(8,128)S(1)}, f32[512]{0:T(512)S(1)}, ...), condition=%wide.region_2.3_spmd.clone, body=%wide.region_0.2_spmd.clone.sunk | while | flops 808059392 | bytes 1089644 | solution.py:39
  10.1 3.8 %fusion.56 = f32[512,128]{1,0:T(8,128)S(1)} fusion(f32[1024]{0:T(1024)S(1)} %bitcast.56, s32[1024]{0:T(1024)S(1)} %bitcast.58, f32[2,1024,128]{2,1,0:T(8,128)S(1)} %get-tuple-element.448, s32[]{:T(128)} %get-tuple-element.435, f32[512,128]{1,0:T(8,128)S(1)} %get-tuple-element.436, pred[]{:T(512)S(6)} %compare.9), kind=kOutput, calls=%fused_computation.5.clone.1 | convolution fusion | flops 806486016 | bytes 1056773 | tf_op jit(solution)/shard_map/while/body/eval_jaxpr/dot_general | solution.py:25
  13.9 0.3 select_reduce_fusion.2
  14.3 3.8 %fusion.56 = f32[512,128]{1,0:T(8,128)S(1)} fusion(f32[1024]{0:T(1024)S(1)} %bitcast.56, s32[1024]{0:T(1024)S(1)} %bitcast.58, f32[2,1024,128]{2,1,0:T(8,128)S(1)} %get-tuple-element.448, s32[]{:T(128)} %get-tuple-element.435, f32[512,128]{1,0:T(8,128)S(1)} %get-tuple-element.436, pred[]{:T(512)S(6)} %compare.9), kind=kOutput, calls=%fused_computation.5.clone.1 | convolution fusion | flops 806486016 | bytes 1056773 | tf_op jit(solution)/shard_map/while/body/eval_jaxpr/dot_general | solution.py:25
  18.1 0.3 select_reduce_fusion.2
  18.5 0.7 copy-done
  19.2 0.0 reduce-scatter.4.cloned.1.call-update
  19.2 0.0 reduce-scatter.6.cloned.1.call-start
  19.2 0.6 convert_reduce_fusion
  19.8 42.2 %psum.50 = f32[]{:T(128)} all-reduce(f32[]{:T(128)} %convert_reduce_fusion), channel_id=1, replica_groups=mesh['grp'=4,'mem'=8] {'grp','mem'}, use_global_device_ids=true, to_apply=%region_9.10 | all-reduce | flops 1 | bytes 8 | tf_op jit(solution)/shard_map/psum | solution.py:83
  62.0 0.6 fusion.38
  63.2 13.0 %all-reduce.2 = f32[512]{0:T(512)S(1)} all-reduce(f32[512]{0:T(512)S(1)} %get-tuple-element.127), channel_id=2, replica_groups=mesh['grp'=4,'mem'=8] {'mem'}, use_global_device_ids=true, to_apply=%region_5.6.clone | all-reduce | flops 512 | bytes 4096
  76.2 0.1 dynamic-slice.3
  77.6 0.0 reduce-scatter.4.cloned.1.call-done
  77.6 18.8 %all-reduce.7 = (f32[64]{0:T(128)S(1)}, f32[64,128]{1,0:T(8,128)S(1)}) all-reduce(f32[64]{0:T(128)S(1)} %dynamic-slice.3, f32[64,128]{1,0:T(8,128)} %reduce-scatter.4.cloned.1.call-done), channel_id=1, replica_groups=mesh['grp'=4,'mem'=8] {'grp'}, use_global_device_ids=true, to_apply=%region_6.7 | all-reduce | flops 8256 | bytes 66048 | tf_op jit(solution)/shard_map/psum | solution.py:90
  96.4 0.1 broadcast_add_fusion.2
  96.5 0.1 slice_divide_fusion.2
  96.6 9.1 %all_gather.19 = f32[512,64]{1,0:T(8,128)S(1)} all-gather(f32[64,64]{1,0:T(8,128)S(1)} %get-tuple-element.274), channel_id=1, replica_groups=mesh['grp'=4,'mem'=8] {'mem'}, dimensions={0}, use_global_device_ids=true | all-gather | bytes 147456 | tf_op jit(solution)/shard_map/all_gather | solution.py:96
  105.7 8.5 %all_gather.20 = f32[512,64]{1,0:T(8,128)S(1)} all-gather(f32[64,64]{1,0:T(8,128)S(1)} %get-tuple-element.275), channel_id=1, replica_groups=mesh['grp'=4,'mem'=8] {'mem'}, dimensions={0}, use_global_device_ids=true | all-gather | bytes 147456 | tf_op jit(solution)/shard_map/all_gather | solution.py:97
  114.2 13.4 %all-reduce = f32[512]{0:T(512)S(1)} all-reduce(f32[512]{0:T(512)S(1)} %get-tuple-element.281), channel_id=1, replica_groups=mesh['grp'=4,'mem'=8] {'mem'}, use_global_device_ids=true, to_apply=%add | all-reduce | flops 512 | bytes 4096
  127.6 0.2 add_reduce_fusion.1
  127.8 0.1 pad_maximum_fusion.1
  127.9 12.2 %while.40 = (s32[]{:T(128)}, f32[512,128]{1,0:T(8,128)}, f32[512]{0:T(512)S(1)}, f32[512]{0:T(512)S(1)}, f32[2,1024,128]{2,1,0:T(8,128)S(1)}, /*index=5*/f32[512...) while((s32[]{:T(128)}, f32[512,128]{1,0:T(8,128)}, ...), condition=%wide.region_14.15_spmd.clone, body=%wide.region_10.14_spmd.clone.sunk | while | flops 1617559040 | bytes 10293372 | solution.py:39
  127.9 2.0 fusion.59
  130.0 0.3 fusion.60
  130.3 0.5 fusion.61
  130.8 2.7 convolution_add_fusion.4
  133.6 2.0 fusion.59
  135.6 0.3 fusion.60
  135.9 0.5 fusion.61
  136.5 3.7 %convolution_add_fusion.4 = f32[512,128]{1,0:T(8,128)} fusion(f32[2,1024,128]{2,1,0:T(8,128)S(1)} %get-tuple-element.475, s32[]{:T(128)} %get-tuple-element.461, f32[1024,512]{0,1:T(8,128)S(1)} %get-tuple-element.415, f32[1024]{0:T(1024)S(1)} %bitcast.52, f32[1024]{0:T(1024)S(1)} %fusion.60, f32[1024]{0:T(1024)S(1)} %get-tuple-element.416, ...), kind=kOutput, calls=%fused_computation.20.clone.1 | convolution fusion | flops 807010304 | bytes 3158021 | tf_op jit(solution)/shard_map/while/body/eval_jaxpr/dot_general | solution.py:25
  140.1 0.0 reduce-scatter.6.cloned.1.call-update
  140.1 0.0 reduce-scatter.8.cloned.1.call-start
  140.2 11.8 %all-reduce.3 = f32[512]{0:T(512)S(1)} all-reduce(f32[512]{0:T(512)S(1)} %get-tuple-element.129), channel_id=4, replica_groups=mesh['grp'=4,'mem'=8] {'mem'}, use_global_device_ids=true, to_apply=%region_17.18.clone | all-reduce | flops 512 | bytes 4096
  152.0 0.1 dynamic-slice.5
  152.1 19.0 %reduce-scatter.6.cloned.1.call-done = f32[64,128]{1,0:T(8,128)} async-done(((f32[512,128]{1,0:T(8,128)}), f32[64,128]{1,0:T(8,128)}) %reduce-scatter.6.cloned.1.call-update) | async-done | bytes 32784 | tf_op jit(solution)/shard_map/reduce_scatter | solution.py:87
  171.1 19.9 %all-reduce.6 = (f32[64]{0:T(128)S(1)}, f32[64,128]{1,0:T(8,128)S(1)}) all-reduce(f32[64]{0:T(128)S(1)} %dynamic-slice.5, f32[64,128]{1,0:T(8,128)} %reduce-scatter.6.cloned.1.call-done), channel_id=1, replica_groups=mesh['grp'=4,'mem'=8] {'grp'}, use_global_device_ids=true, to_apply=%region_18.19 | all-reduce | flops 8256 | bytes 66048 | tf_op jit(solution)/shard_map/psum | solution.py:90
  191.0 0.1 broadcast_add_fusion.1
  191.1 0.1 slice_divide_fusion.1
  191.2 9.3 %all_gather.22 = f32[512,64]{1,0:T(8,128)S(1)} all-gather(f32[64,64]{1,0:T(8,128)S(1)} %get-tuple-element.272), channel_id=1, replica_groups=mesh['grp'=4,'mem'=8] {'mem'}, dimensions={0}, use_global_device_ids=true | all-gather | bytes 147456 | tf_op jit(solution)/shard_map/all_gather | solution.py:96
  200.4 8.3 %all_gather.23 = f32[512,64]{1,0:T(8,128)S(1)} all-gather(f32[64,64]{1,0:T(8,128)S(1)} %get-tuple-element.273), channel_id=1, replica_groups=mesh['grp'=4,'mem'=8] {'mem'}, dimensions={0}, use_global_device_ids=true | all-gather | bytes 147456 | tf_op jit(solution)/shard_map/all_gather | solution.py:97
  208.8 13.4 %all-reduce.1 = f32[512]{0:T(512)S(1)} all-reduce(f32[512]{0:T(512)S(1)} %get-tuple-element.279), channel_id=1, replica_groups=mesh['grp'=4,'mem'=8] {'mem'}, use_global_device_ids=true, to_apply=%add.1 | all-reduce | flops 512 | bytes 4096
  222.2 0.2 add_reduce_fusion
  222.3 0.1 pad_maximum_fusion.2
  222.5 12.2 %while.41 = (s32[]{:T(128)}, f32[512,128]{1,0:T(8,128)}, f32[512]{0:T(512)S(1)}, f32[512]{0:T(512)S(1)}, f32[2,1024,128]{2,1,0:T(8,128)S(1)}, /*index=5*/f32[512...) while((s32[]{:T(128)}, f32[512,128]{1,0:T(8,128)}, ...), condition=%wide.region_24.25_spmd.clone, body=%wide.region_20.24_spmd.clone.sunk | while | flops 1617559040 | bytes 10293372 | solution.py:39
  222.5 2.0 fusion.64
  224.6 0.3 fusion.65
  224.9 0.5 fusion.66
  225.4 2.7 convolution_add_fusion.5
  228.2 2.0 fusion.64
  230.2 0.3 fusion.65
  230.5 0.5 fusion.66
  231.1 3.7 %convolution_add_fusion.5 = f32[512,128]{1,0:T(8,128)} fusion(f32[2,1024,128]{2,1,0:T(8,128)S(1)} %get-tuple-element.505, s32[]{:T(128)} %get-tuple-element.491, f32[1024,512]{0,1:T(8,128)S(1)} %get-tuple-element.425, f32[1024]{0:T(1024)S(1)} %bitcast.55, f32[1024]{0:T(1024)S(1)} %fusion.65, f32[1024]{0:T(1024)S(1)} %get-tuple-element.426, ...), kind=kOutput, calls=%fused_computation.35.clone.1 | convolution fusion | flops 807010304 | bytes 3158021 | tf_op jit(solution)/shard_map/while/body/eval_jaxpr/dot_general | solution.py:25
  234.7 0.0 reduce-scatter.8.cloned.1.call-update
  234.7 11.8 %all-reduce.4 = f32[512]{0:T(512)S(1)} all-reduce(f32[512]{0:T(512)S(1)} %get-tuple-element.132), channel_id=7, replica_groups=mesh['grp'=4,'mem'=8] {'mem'}, use_global_device_ids=true, to_apply=%region_27.28.clone | all-reduce | flops 512 | bytes 4096
  246.5 0.1 dynamic-slice.7
  246.6 19.2 %reduce-scatter.8.cloned.1.call-done = f32[64,128]{1,0:T(8,128)} async-done(((f32[512,128]{1,0:T(8,128)}), f32[64,128]{1,0:T(8,128)}) %reduce-scatter.8.cloned.1.call-update) | async-done | bytes 32784 | tf_op jit(solution)/shard_map/reduce_scatter | solution.py:87
  265.8 19.9 %all-reduce.5 = (f32[64,128]{1,0:T(8,128)S(1)}, f32[64]{0:T(128)S(1)}) all-reduce(f32[64,128]{1,0:T(8,128)} %reduce-scatter.8.cloned.1.call-done, f32[64]{0:T(128)S(1)} %dynamic-slice.7), channel_id=1, replica_groups=mesh['grp'=4,'mem'=8] {'grp'}, use_global_device_ids=true, to_apply=%region_26.27 | all-reduce | flops 8256 | bytes 66048 | tf_op jit(solution)/shard_map/psum | solution.py:90
  285.7 0.5 broadcast_divide_fusion.2
  286.2 0.7 fusion.31
  (37 shorter events, 0.2 us)
Async XLA Ops:
  7.2 70.4 %reduce-scatter.4.cloned.1.call-start = ((), (), s32[]{:S(2)}) async-start(), calls=%async_computation.3 | async-start | bytes 294912 | tf_op jit(solution)/shard_map/reduce_scatter | solution.py:87
  8.5 1.5 copy-start.2
  8.5 1.5 copy-start.1
  10.1 51.9 %copy-start.3 = (u32[32]{0:T(128)S(1)}, u32[32]{0:T(128)}, u32[]{:S(2)}) copy-start(u32[32]{0:T(128)} %constant.58) | copy-start | bytes 388
  18.5 0.7 copy-start
  19.2 151.9 %reduce-scatter.6.cloned.1.call-start = ((), (), s32[]{:S(2)}) async-start(), calls=%async_computation.4 | async-start | bytes 294912 | tf_op jit(solution)/shard_map/reduce_scatter | solution.py:87
  140.1 125.7 %reduce-scatter.8.cloned.1.call-start = ((), (), s32[]{:S(2)}) async-start(), calls=%async_computation.5 | async-start | bytes 294912 | tf_op jit(solution)/shard_map/reduce_scatter | solution.py:87
Sparse Core Ops, SparseCore 0:
  19.3 36.3 reduce-scatter.3
  140.3 30.7 reduce-scatter.5
  234.9 30.9 reduce-scatter.7
where the time goes:
time: 294 us; the launch traced here: 293 us
  blocking collectives  199 us (68%)
  waiting for transfers between devices  38.3 us (13%)
  matrix products  28.4 us (10%)
  between operations  15.9 us (5%)
  other arithmetic  9.37 us (3%)
    unnamed x5, blocking collectives  63.3 us
    psum x3, blocking collectives, combine(): return lax.psum((shared[0], shared[1]), 'grp')  58.5 us
    psum x1, blocking collectives, shards(): total = lax.psum(jnp.sum(virtual), ('grp', 'mem'))  42.2 us
    reduce_scatter x3, waiting for transfers between devices, combine(): lax.psum_scatter(local_sums, 'mem', scatter_dimension=0, tiled=True)  38.2 us
    dot_general x6, matrix products, advance(): lax.dot_general(weights, piece[0], (((0,), (0,)), ((), ())), precision=la...  20.3 us
    all_gather x2, blocking collectives, shards(): lax.all_gather(means, 'mem', axis=0, tiled=True)  18.4 us
    all_gather x2, blocking collectives, shards(): lax.all_gather(variances, 'mem', axis=0, tiled=True)  16.8 us
    dot_general x4, matrix products, soft_weights(): lax.dot_general(block_features, table, (((1,), (1,)), ((), ())), precisio...  8.14 us
  transfers between devices with their start and end apart: 3, of which 2 were waited for; matrix products, arithmetic and copies ran while one was open for 0% of the time, Pallas kernels for 0%

commit v1 on v0

--- a/solution.py
+++ b/solution.py
@@ -6,6 +6,19 @@
 
 P_SIZE = 512
 ITERS = 2
+
+
+def ring_gather(x, axis, dim):
+    ways = lax.axis_size(axis)
+    up = [(d, (d + 1) % ways) for d in range(ways)]
+    down = [(d, (d - 1) % ways) for d in range(ways)]
+    earlier, later = ([x], [x])
+    for _ in range(ways // 2):
+        earlier.append(lax.ppermute(earlier[-1], axis, up))
+    for _ in range((ways - 1) // 2):
+        later.append(lax.ppermute(later[-1], axis, down))
+    line = jnp.concatenate([*earlier[::-1], *later[1:]], axis=dim)
+    return jnp.roll(line, (lax.axis_index(axis) - ways // 2) * x.shape[dim], axis=dim)
 
 
 def child_features(means, variances):
@@ -94,7 +107,7 @@
     for iteration in range(ITERS):
         all_means, all_variances, all_weights = (
             lax.all_gather(means, "mem", axis=0, tiled=True),
-            lax.all_gather(variances, "mem", axis=0, tiled=True),
+            ring_gather(variances, "mem", 0),
             lax.all_gather(weights, "mem", axis=0, tiled=True),
         )
         table, offset, log_weight = parent_table(all_means, all_variances, all_weights)

time: 294 us -> 307 us (1.044)
  waiting for transfers between devices: 38.3 us -> 50.7 us
  starting transfers between devices: 0.12 us -> 9.94 us
  blocking collectives: 199 us -> 190 us
    all_gather x2 -> x0, blocking collectives: 16.8 us -> none  [shards(): lax.all_gather(variances, 'mem', axis=0, tiled=True)]
    ppermute x0 -> x14, waiting for transfers between devices: none -> 15 us  [the longest x8 11.9 us: ring_gather(): earlier.append(lax.ppermute(earlier[-1], axis, up))]
    ppermute x0 -> x14, starting transfers between devices: none -> 9.82 us  [the longest x6 8.72 us: ring_gather(): later.append(lax.ppermute(later[-1], axis, down))]
    unnamed x5, blocking collectives: 63.3 us -> 70.6 us
  transfers between devices with their start and end apart: 3 -> 17, of which waited for: 2 -> 8; matrix products, arithmetic and copies ran while one was open for 0% -> 0% of each run, Pallas kernels for 0% -> 0%
where the time goes in v1:
time: 307 us; the launch traced here: 306 us
  blocking collectives  190 us (62%)
  waiting for transfers between devices  50.7 us (17%)
  matrix products  28.4 us (9%)
  between operations  16 us (5%)
  starting transfers between devices  9.94 us (3%)
  other arithmetic  9.59 us (3%)
    unnamed x5, blocking collectives  70.6 us
    psum x3, blocking collectives, combine(): return lax.psum((shared[0], shared[1]), 'grp')  58.4 us
    psum x1, blocking collectives, shards(): total = lax.psum(jnp.sum(virtual), ('grp', 'mem'))  42.2 us
    reduce_scatter x3, waiting for transfers between devices, combine(): lax.psum_scatter(local_sums, 'mem', scatter_dimension=0, tiled=True)  35.6 us
    dot_general x6, matrix products, advance(): lax.dot_general(weights, piece[0], (((0,), (0,)), ((), ())), precision=la...  20.3 us
    all_gather x2, blocking collectives, shards(): lax.all_gather(means, 'mem', axis=0, tiled=True)  18.4 us
    ppermute x8, waiting for transfers between devices, ring_gather(): earlier.append(lax.ppermute(earlier[-1], axis, up))  11.9 us
    ppermute x6, starting transfers between devices, ring_gather(): later.append(lax.ppermute(later[-1], axis, down))  8.72 us
  transfers between devices with their start and end apart: 17, of which 8 were waited for; matrix products, arithmetic and copies ran while one was open for 0% of the time, Pallas kernels for 0%

profile of v1, /device:TPU:0, one launch (start us, length us, event | category | flops | bytes accessed | tf_op | source)
XLA Modules:
  0.0 306.5 jit_solution(6520299033157806422)
XLA Ops:
  7.2 1.3 multiply_add_fusion.2
  8.5 1.2 pad_maximum_fusion
  9.7 0.3 copy.9
  10.1 8.4 %while.39 = (s32[]{:T(128)}, f32[512,128]{1,0:T(8,128)S(1)}, f32[512]{0:T(512)S(1)}, s32[2,1024,1]{1,2,0:T(1,128)S(1)}, f32[2,1024]{1,0:T(2,128)S(1)}, /*index=5*/f32[2,1024,128]{2,1,0:T(8,128)S(1)}, s32[]{:T(128)}, s32[]{:T(128)}) while((s32[]{:T(128)}, f32[512,128]{1,0:T(8,128)S(1)}, f32[512]{0:T(512)S(1)}, ...), condition=%wide.region_2.3_spmd.clone, body=%wide.region_0.2_spmd.clone.sunk | while | flops 808059392 | bytes 1089644 | solution.py:52
  10.1 3.8 %fusion.58 = f32[512,128]{1,0:T(8,128)S(1)} fusion(f32[1024]{0:T(1024)S(1)} %bitcast.56, s32[1024]{0:T(1024)S(1)} %bitcast.58, f32[2,1024,128]{2,1,0:T(8,128)S(1)} %get-tuple-element.447, s32[]{:T(128)} %get-tuple-element.434, f32[512,128]{1,0:T(8,128)S(1)} %get-tuple-element.435, pred[]{:T(512)S(6)} %compare.10), kind=kOutput, calls=%fused_computation.5.clone.1 | convolution fusion | flops 806486016 | bytes 1056773 | tf_op jit(solution)/shard_map/while/body/eval_jaxpr/dot_general | solution.py:38
  13.9 0.3 select_reduce_fusion.2
  14.3 3.8 %fusion.58 = f32[512,128]{1,0:T(8,128)S(1)} fusion(f32[1024]{0:T(1024)S(1)} %bitcast.56, s32[1024]{0:T(1024)S(1)} %bitcast.58, f32[2,1024,128]{2,1,0:T(8,128)S(1)} %get-tuple-element.447, s32[]{:T(128)} %get-tuple-element.434, f32[512,128]{1,0:T(8,128)S(1)} %get-tuple-element.435, pred[]{:T(512)S(6)} %compare.10), kind=kOutput, calls=%fused_computation.5.clone.1 | convolution fusion | flops 806486016 | bytes 1056773 | tf_op jit(solution)/shard_map/while/body/eval_jaxpr/dot_general | solution.py:38
  18.1 0.3 select_reduce_fusion.2
  18.5 0.7 copy-done
  19.2 0.6 convert_reduce_fusion
  19.8 42.2 %psum.50 = f32[]{:T(128)} all-reduce(f32[]{:T(128)} %convert_reduce_fusion), channel_id=1, replica_groups=mesh['grp'=4,'mem'=8] {'grp','mem'}, use_global_device_ids=true, to_apply=%region_9.11 | all-reduce | flops 1 | bytes 8 | tf_op jit(solution)/shard_map/psum | solution.py:96
  62.0 0.6 fusion.40
  63.2 12.9 %all-reduce.2 = f32[512]{0:T(512)S(1)} all-reduce(f32[512]{0:T(512)S(1)} %get-tuple-element.128), channel_id=2, replica_groups=mesh['grp'=4,'mem'=8] {'mem'}, use_global_device_ids=true, to_apply=%region_5.6.clone | all-reduce | flops 512 | bytes 4096
  77.5 18.7 %all-reduce.7 = (f32[64]{0:T(128)S(1)}, f32[64,128]{1,0:T(8,128)S(1)}) all-reduce(f32[64]{0:T(128)S(1)} %dynamic-slice.3, f32[64,128]{1,0:T(8,128)} %reduce-scatter.4.cloned.1.call-done), channel_id=1, replica_groups=mesh['grp'=4,'mem'=8] {'grp'}, use_global_device_ids=true, to_apply=%region_6.7 | all-reduce | flops 8256 | bytes 66048 | tf_op jit(solution)/shard_map/psum | solution.py:103
  96.3 0.1 broadcast_add_fusion.2
  96.4 0.1 fusion.37
  96.5 4.2 %collective-permute-done = f32[64,64]{1,0:T(8,128)S(1)} collective-permute-done((f32[64,64]{1,0:T(8,128)S(1)}, f32[64,64]{1,0:T(8,128)S(1)}, u32[]{:S(2)}, u32[]{:S(2)}) %collective-permute-start) | collective-permute-done | bytes 16416 | tf_op jit(solution)/shard_map/ppermute | solution.py:17
  100.8 2.6 collective-permute-start.4
  103.4 1.6 collective-permute-done.1
  105.0 14.4 %all-reduce = f32[512]{0:T(512)S(1)} all-reduce(f32[512]{0:T(512)S(1)} %get-tuple-element.280), channel_id=1, replica_groups=mesh['grp'=4,'mem'=8] {'mem'}, use_global_device_ids=true, to_apply=%add | all-reduce | flops 512 | bytes 4096
  119.5 0.5 collective-permute-start.3
  120.0 9.2 %all_gather.13 = f32[512,64]{1,0:T(8,128)S(1)} all-gather(f32[64,64]{1,0:T(8,128)S(1)} %get-tuple-element.274), channel_id=1, replica_groups=mesh['grp'=4,'mem'=8] {'mem'}, dimensions={0}, use_global_device_ids=true | all-gather | bytes 147456 | tf_op jit(solution)/shard_map/all_gather | solution.py:109
  129.2 1.6 collective-permute-start.6
  130.9 1.5 collective-permute-done.6
  132.4 0.3 add_reduce_fusion.1
  132.7 0.1 pad_maximum_fusion.1
  132.8 12.2 %while.40 = (s32[]{:T(128)}, f32[512,128]{1,0:T(8,128)}, f32[512]{0:T(512)S(1)}, f32[512]{0:T(512)S(1)}, f32[2,1024,128]{2,1,0:T(8,128)S(1)}, /*index=5*/f32[512...) while((s32[]{:T(128)}, f32[512,128]{1,0:T(8,128)}, ...), condition=%wide.region_14.16_spmd.clone, body=%wide.region_10.15_spmd.clone.sunk | while | flops 1617559040 | bytes 10293372 | solution.py:52
  132.9 2.0 fusion.61
  134.9 0.3 fusion.62
  135.3 0.5 fusion.63
  135.8 2.7 convolution_add_fusion.4
  138.5 2.0 fusion.61
  140.6 0.3 fusion.62
  140.9 0.5 fusion.63
  141.4 3.7 %convolution_add_fusion.4 = f32[512,128]{1,0:T(8,128)} fusion(f32[2,1024,128]{2,1,0:T(8,128)S(1)} %get-tuple-element.474, s32[]{:T(128)} %get-tuple-element.460, f32[1024,512]{0,1:T(8,128)S(1)} %get-tuple-element.414, f32[1024]{0:T(1024)S(1)} %bitcast.52, f32[1024]{0:T(1024)S(1)} %fusion.62, f32[1024]{0:T(1024)S(1)} %get-tuple-element.415, ...), kind=kOutput, calls=%fused_computation.20.clone.1 | convolution fusion | flops 807010304 | bytes 3158021 | tf_op jit(solution)/shard_map/while/body/eval_jaxpr/dot_general | solution.py:38
  145.2 14.4 %all-reduce.3 = f32[512]{0:T(512)S(1)} all-reduce(f32[512]{0:T(512)S(1)} %get-tuple-element.130), channel_id=4, replica_groups=mesh['grp'=4,'mem'=8] {'mem'}, use_global_device_ids=true, to_apply=%region_17.19.clone | all-reduce | flops 512 | bytes 4096
  159.7 17.8 %reduce-scatter.6.cloned.1.call-done = f32[64,128]{1,0:T(8,128)} async-done(((f32[512,128]{1,0:T(8,128)}), f32[64,128]{1,0:T(8,128)}) %reduce-scatter.6.cloned.1.call-update) | async-done | bytes 32784 | tf_op jit(solution)/shard_map/reduce_scatter | solution.py:100
  177.4 19.8 %all-reduce.6 = (f32[64]{0:T(128)S(1)}, f32[64,128]{1,0:T(8,128)S(1)}) all-reduce(f32[64]{0:T(128)S(1)} %dynamic-slice.5, f32[64,128]{1,0:T(8,128)} %reduce-scatter.6.cloned.1.call-done), channel_id=1, replica_groups=mesh['grp'=4,'mem'=8] {'grp'}, use_global_device_ids=true, to_apply=%region_18.20 | all-reduce | flops 8256 | bytes 66048 | tf_op jit(solution)/shard_map/psum | solution.py:103
  197.3 0.1 broadcast_add_fusion.1
  197.4 0.1 fusion.35
  197.6 4.2 %collective-permute-done.7 = f32[64,64]{1,0:T(8,128)S(1)} collective-permute-done((f32[64,64]{1,0:T(8,128)S(1)}, f32[64,64]{1,0:T(8,128)S(1)}, u32[]{:S(2)}, u32[]{:S(2)}) %collective-permute-start.7) | collective-permute-done | bytes 16416 | tf_op jit(solution)/shard_map/ppermute | solution.py:17
  201.8 2.6 collective-permute-start.11
  204.4 1.9 collective-permute-done.8
  206.3 14.4 %all-reduce.1 = f32[512]{0:T(512)S(1)} all-reduce(f32[512]{0:T(512)S(1)} %get-tuple-element.278), channel_id=1, replica_groups=mesh['grp'=4,'mem'=8] {'mem'}, use_global_device_ids=true, to_apply=%add.1 | all-reduce | flops 512 | bytes 4096
  220.8 0.5 collective-permute-start.10
  221.3 9.3 %all_gather.15 = f32[512,64]{1,0:T(8,128)S(1)} all-gather(f32[64,64]{1,0:T(8,128)S(1)} %get-tuple-element.272), channel_id=1, replica_groups=mesh['grp'=4,'mem'=8] {'mem'}, dimensions={0}, use_global_device_ids=true | all-gather | bytes 147456 | tf_op jit(solution)/shard_map/all_gather | solution.py:109
  230.6 1.7 collective-permute-start.13
  232.3 1.5 collective-permute-done.13
  233.9 0.3 add_reduce_fusion
  234.2 0.1 pad_maximum_fusion.2
  234.3 12.2 %while.41 = (s32[]{:T(128)}, f32[512,128]{1,0:T(8,128)}, f32[512]{0:T(512)S(1)}, f32[512]{0:T(512)S(1)}, f32[2,1024,128]{2,1,0:T(8,128)S(1)}, /*index=5*/f32[512...) while((s32[]{:T(128)}, f32[512,128]{1,0:T(8,128)}, ...), condition=%wide.region_24.26_spmd.clone, body=%wide.region_20.25_spmd.clone.sunk | while | flops 1617559040 | bytes 10293372 | solution.py:52
  234.3 2.0 fusion.66
  236.4 0.3 fusion.67
  236.7 0.5 fusion.68
  237.2 2.7 convolution_add_fusion.5
  240.0 2.0 fusion.66
  242.0 0.3 fusion.67
  242.4 0.5 fusion.68
  242.9 3.7 %convolution_add_fusion.5 = f32[512,128]{1,0:T(8,128)} fusion(f32[2,1024,128]{2,1,0:T(8,128)S(1)} %get-tuple-element.504, s32[]{:T(128)} %get-tuple-element.490, f32[1024,512]{0,1:T(8,128)S(1)} %get-tuple-element.424, f32[1024]{0:T(1024)S(1)} %bitcast.55, f32[1024]{0:T(1024)S(1)} %fusion.67, f32[1024]{0:T(1024)S(1)} %get-tuple-element.425, ...), kind=kOutput, calls=%fused_computation.35.clone.1 | convolution fusion | flops 807010304 | bytes 3158021 | tf_op jit(solution)/shard_map/while/body/eval_jaxpr/dot_general | solution.py:38
  246.6 14.4 %all-reduce.4 = f32[512]{0:T(512)S(1)} all-reduce(f32[512]{0:T(512)S(1)} %get-tuple-element.133), channel_id=7, replica_groups=mesh['grp'=4,'mem'=8] {'mem'}, use_global_device_ids=true, to_apply=%region_27.29.clone | all-reduce | flops 512 | bytes 4096
  261.1 17.8 %reduce-scatter.8.cloned.1.call-done = f32[64,128]{1,0:T(8,128)} async-done(((f32[512,128]{1,0:T(8,128)}), f32[64,128]{1,0:T(8,128)}) %reduce-scatter.8.cloned.1.call-update) | async-done | bytes 32784 | tf_op jit(solution)/shard_map/reduce_scatter | solution.py:100
  278.9 19.8 %all-reduce.5 = (f32[64,128]{1,0:T(8,128)S(1)}, f32[64]{0:T(128)S(1)}) all-reduce(f32[64,128]{1,0:T(8,128)} %reduce-scatter.8.cloned.1.call-done, f32[64]{0:T(128)S(1)} %dynamic-slice.7), channel_id=1, replica_groups=mesh['grp'=4,'mem'=8] {'grp'}, use_global_device_ids=true, to_apply=%region_26.28 | all-reduce | flops 8256 | bytes 66048 | tf_op jit(solution)/shard_map/psum | solution.py:103
  298.7 0.5 broadcast_divide_fusion.2
  299.2 0.7 fusion.33
  (81 shorter events, 1.0 us)
Async XLA Ops:
  7.2 70.4 %reduce-scatter.4.cloned.1.call-start = ((), (), s32[]{:S(2)}) async-start(), calls=%async_computation.3 | async-start | bytes 294912 | tf_op jit(solution)/shard_map/reduce_scatter | solution.py:100
  8.5 1.5 copy-start.2
  8.5 1.6 copy-start.1
  10.1 51.9 %copy-start.3 = (u32[32]{0:T(128)S(1)}, u32[32]{0:T(128)}, u32[]{:S(2)}) copy-start(u32[32]{0:T(128)} %constant.84) | copy-start | bytes 388
  18.5 0.7 copy-start
  19.2 158.3 %reduce-scatter.6.cloned.1.call-start = ((), (), s32[]{:S(2)}) async-start(), calls=%async_computation.4 | async-start | bytes 294912 | tf_op jit(solution)/shard_map/reduce_scatter | solution.py:100
  96.5 4.3 %collective-permute-start = (f32[64,64]{1,0:T(8,128)S(1)}, f32[64,64]{1,0:T(8,128)S(1)}, u32[]{:S(2)}, u32[]{:S(2)}) collective-permute-start(f32[64,64]{1,0:T(8,128)S(1)} %get-tuple-element.273), channel_id=1, source_target_pairs={{0,1},{1,2},{2,3},{3,4},{4,5},{5,6},{6,7},{7,0},{8,9},{9,10},{10,1... | collective-permute-start | bytes 49160 | tf_op jit(solution)/shard_map/ppermute | solution.py:17
  100.8 4.2 %collective-permute-start.1 = (f32[64,64]{1,0:T(8,128)S(1)}, f32[64,64]{1,0:T(8,128)S(1)}, u32[]{:S(2)}, u32[]{:S(2)}) collective-permute-start(f32[64,64]{1,0:T(8,128)S(1)} %collective-permute-done), channel_id=1, source_target_pairs={{0,1},{1,2},{2,3},{3,4},{4,5},{5,6},{6,7},{7,0},{8,9},{9,10},{10,1... | collective-permute-start | bytes 49160 | tf_op jit(solution)/shard_map/ppermute | solution.py:17
  100.8 18.7 %collective-permute-start.4 = (f32[64,64]{1,0:T(8,128)S(1)}, f32[64,64]{1,0:T(8,128)S(1)}, u32[]{:S(2)}, u32[]{:S(2)}) collective-permute-start(f32[64,64]{1,0:T(8,128)S(1)} %get-tuple-element.273), channel_id=1, source_target_pairs={{0,7},{1,0},{2,1},{3,2},{4,3},{5,4},{6,5},{7,6},{8,15},{9,8},{10,9... | collective-permute-start | bytes 49160 | tf_op jit(solution)/shard_map/ppermute | solution.py:19
  105.0 14.5 %collective-permute-start.2 = (f32[64,64]{1,0:T(8,128)S(1)}, f32[64,64]{1,0:T(8,128)S(1)}, u32[]{:S(2)}, u32[]{:S(2)}) collective-permute-start(f32[64,64]{1,0:T(8,128)S(1)} %collective-permute-done.1), channel_id=1, source_target_pairs={{0,1},{1,2},{2,3},{3,4},{4,5},{5,6},{6,7},{7,0},{8,9},{9,10},{10,1... | collective-permute-start | bytes 49160 | tf_op jit(solution)/shard_map/ppermute | solution.py:17
  119.4 9.7 %collective-permute-start.5 = (f32[64,64]{1,0:T(8,128)S(1)}, f32[64,64]{1,0:T(8,128)S(1)}, u32[]{:S(2)}, u32[]{:S(2)}) collective-permute-start(f32[64,64]{1,0:T(8,128)S(1)} %collective-permute-done.4), channel_id=1, source_target_pairs={{0,7},{1,0},{2,1},{3,2},{4,3},{5,4},{6,5},{7,6},{8,15},{9,8},{10,9... | collective-permute-start | bytes 49160 | tf_op jit(solution)/shard_map/ppermute | solution.py:19
  119.5 11.3 %collective-permute-start.3 = (f32[64,64]{1,0:T(8,128)S(1)}, f32[64,64]{1,0:T(8,128)S(1)}, u32[]{:S(2)}, u32[]{:S(2)}) collective-permute-start(f32[64,64]{1,0:T(8,128)S(1)} %collective-permute-done.2), channel_id=1, source_target_pairs={{0,1},{1,2},{2,3},{3,4},{4,5},{5,6},{6,7},{7,0},{8,9},{9,10},{10,1... | collective-permute-start | bytes 49160 | tf_op jit(solution)/shard_map/ppermute | solution.py:17
  129.2 3.2 %collective-permute-start.6 = (f32[64,64]{1,0:T(8,128)S(1)}, f32[64,64]{1,0:T(8,128)S(1)}, u32[]{:S(2)}, u32[]{:S(2)}) collective-permute-start(f32[64,64]{1,0:T(8,128)S(1)} %collective-permute-done.5), channel_id=1, source_target_pairs={{0,7},{1,0},{2,1},{3,2},{4,3},{5,4},{6,5},{7,6},{8,15},{9,8},{10,9... | collective-permute-start | bytes 49160 | tf_op jit(solution)/shard_map/ppermute | solution.py:19
  145.1 133.8 %reduce-scatter.8.cloned.1.call-start = ((), (), s32[]{:S(2)}) async-start(), calls=%async_computation.5 | async-start | bytes 294912 | tf_op jit(solution)/shard_map/reduce_scatter | solution.py:100
  197.5 4.3 %collective-permute-start.7 = (f32[64,64]{1,0:T(8,128)S(1)}, f32[64,64]{1,0:T(8,128)S(1)}, u32[]{:S(2)}, u32[]{:S(2)}) collective-permute-start(f32[64,64]{1,0:T(8,128)S(1)} %get-tuple-element.271), channel_id=1, source_target_pairs={{0,1},{1,2},{2,3},{3,4},{4,5},{5,6},{6,7},{7,0},{8,9},{9,10},{10,1... | collective-permute-start | bytes 49160 | tf_op jit(solution)/shard_map/ppermute | solution.py:17
  201.8 4.5 %collective-permute-start.8 = (f32[64,64]{1,0:T(8,128)S(1)}, f32[64,64]{1,0:T(8,128)S(1)}, u32[]{:S(2)}, u32[]{:S(2)}) collective-permute-start(f32[64,64]{1,0:T(8,128)S(1)} %collective-permute-done.7), channel_id=1, source_target_pairs={{0,1},{1,2},{2,3},{3,4},{4,5},{5,6},{6,7},{7,0},{8,9},{9,10},{10,1... | collective-permute-start | bytes 49160 | tf_op jit(solution)/shard_map/ppermute | solution.py:17
  201.8 19.0 %collective-permute-start.11 = (f32[64,64]{1,0:T(8,128)S(1)}, f32[64,64]{1,0:T(8,128)S(1)}, u32[]{:S(2)}, u32[]{:S(2)}) collective-permute-start(f32[64,64]{1,0:T(8,128)S(1)} %get-tuple-element.271), channel_id=1, source_target_pairs={{0,7},{1,0},{2,1},{3,2},{4,3},{5,4},{6,5},{7,6},{8,15},{9,8},{10,9... | collective-permute-start | bytes 49160 | tf_op jit(solution)/shard_map/ppermute | solution.py:19
  206.3 14.5 %collective-permute-start.9 = (f32[64,64]{1,0:T(8,128)S(1)}, f32[64,64]{1,0:T(8,128)S(1)}, u32[]{:S(2)}, u32[]{:S(2)}) collective-permute-start(f32[64,64]{1,0:T(8,128)S(1)} %collective-permute-done.8), channel_id=1, source_target_pairs={{0,1},{1,2},{2,3},{3,4},{4,5},{5,6},{6,7},{7,0},{8,9},{9,10},{10,1... | collective-permute-start | bytes 49160 | tf_op jit(solution)/shard_map/ppermute | solution.py:17
  220.8 9.8 %collective-permute-start.12 = (f32[64,64]{1,0:T(8,128)S(1)}, f32[64,64]{1,0:T(8,128)S(1)}, u32[]{:S(2)}, u32[]{:S(2)}) collective-permute-start(f32[64,64]{1,0:T(8,128)S(1)} %collective-permute-done.11), channel_id=1, source_target_pairs={{0,7},{1,0},{2,1},{3,2},{4,3},{5,4},{6,5},{7,6},{8,15},{9,8},{10,9... | collective-permute-start | bytes 49160 | tf_op jit(solution)/shard_map/ppermute | solution.py:19
  220.8 11.4 %collective-permute-start.10 = (f32[64,64]{1,0:T(8,128)S(1)}, f32[64,64]{1,0:T(8,128)S(1)}, u32[]{:S(2)}, u32[]{:S(2)}) collective-permute-start(f32[64,64]{1,0:T(8,128)S(1)} %collective-permute-done.9), channel_id=1, source_target_pairs={{0,1},{1,2},{2,3},{3,4},{4,5},{5,6},{6,7},{7,0},{8,9},{9,10},{10,1... | collective-permute-start | bytes 49160 | tf_op jit(solution)/shard_map/ppermute | solution.py:17
  230.6 3.3 %collective-permute-start.13 = (f32[64,64]{1,0:T(8,128)S(1)}, f32[64,64]{1,0:T(8,128)S(1)}, u32[]{:S(2)}, u32[]{:S(2)}) collective-permute-start(f32[64,64]{1,0:T(8,128)S(1)} %collective-permute-done.12), channel_id=1, source_target_pairs={{0,7},{1,0},{2,1},{3,2},{4,3},{5,4},{6,5},{7,6},{8,15},{9,8},{10,9... | collective-permute-start | bytes 49160 | tf_op jit(solution)/shard_map/ppermute | solution.py:19
Sparse Core Ops, SparseCore 0:
  19.3 36.3 reduce-scatter.3
  145.2 32.1 reduce-scatter.5
  246.7 32.1 reduce-scatter.7
